TPU v7x, 256 devices: a whole 4x4x8 slice. The times are simulated.
256 devices in a mesh: tile: 16 (over y, z_hi), head: 16 (over x, z_lo, core).
Axes of the slice: x: 4, y: 4, z: 8 (z_hi: 4, z_lo: 2; z = z_hi * 2 + z_lo), core: 2. Of those that a mesh axis runs over, the one named last changes fastest.
Arguments:
- tokens: bfloat16 [6144, 3072], P('tile'), may hold values from -200 to 200
- mod_shift: float32 [3072], replicated, may hold values from -3 to 3
- mod_scale: float32 [3072], replicated, may hold values from -2.5 to 2.5
- mod_gate: float32 [3072], replicated, may hold values from -4 to 4
- qkv_weight: bfloat16 [3072, 6144], P(None, 'head'), may hold values from -1 to 1
- out_weight: bfloat16 [2048, 3072], P('head'), may hold values from -0.125 to 0.125
- teacher: bfloat16 [6144, 3072], P('tile'), may hold values from -6 to 6
- slot_tiles: int32 [16], replicated, may hold values from 0 to 15, each once
Outputs:
- qkv_grad: float32 [3072, 6144], P('tile', 'head')
- out_grad: float32 [2048, 3072], P('head', 'tile')
Inputs may be any that keep to these rules, and one draw needn't show every extreme that they name: Slot s, rows s * 384 to (s + 1) * 384 - 1 of tokens and teacher, holds tile slot_tiles[s]; every tile once.
All inputs are finite; a program needn't handle non-finite values.
Results may differ from a plain program's by a relative error of at most 0.00049.
Values may be sent and summed in bfloat16 or wider, within the bound.
A program may use at most 128 MiB of HBM per device.

v0:
```python
import math
import jax
import jax.numpy as jnp
from jax import lax
from jax.sharding import PartitionSpec as P

HD = 128
TOK_TILE = 384
TT = 1
TH = 4
EPS_NORM = 1e-05
EPS_ROOT = 1e-06
LOSS_WEIGHT = 32.0


def modulated_norm(tokens, mod_shift, mod_scale):
    values_in = tokens.astype(jnp.float32)
    center = values_in - jnp.mean(values_in, -1, keepdims=True)
    spread = jnp.mean(center * center, -1, keepdims=True)
    return (center * lax.rsqrt(spread + EPS_NORM) * (1.0 + mod_scale) + mod_shift).astype(
        jnp.bfloat16
    )


def root_norm(values):
    factor = lax.rsqrt(jnp.mean(values * values, -1, keepdims=True) + EPS_ROOT)
    return (values * factor, factor)


def root_norm_back(grad_unit, unit_value, factor):
    return factor * (grad_unit - unit_value * jnp.mean(grad_unit * unit_value, -1, keepdims=True))


def tiles_of(slot_tiles, slot_ids):
    onehot = (
        slot_ids[:, None] == jnp.arange(slot_tiles.shape[0], dtype=jnp.int32)[None, :]
    ).astype(jnp.int32)
    return jnp.sum(onehot * slot_tiles[None, :], 1)


def near_tiles(first_tiles, second_tiles, width_tiles):

    def coords(ids):
        return (ids // (TH * width_tiles), ids // width_tiles % TH, ids % width_tiles)

    ta, ha, wa = coords(first_tiles[:, None])
    tb, hb, wb = coords(second_tiles[None, :])
    close = (jnp.abs(ta - tb) <= 1) & (jnp.abs(ha - hb) <= 1) & (jnp.abs(wa - wb) <= 1)
    return close.astype(jnp.float32)


def masked_exp(queries, keys, tile_mask, group_rows):
    att_scale = 1.0 / math.sqrt(HD)
    scores = (
        jnp.einsum("qhd,khd->hqk", queries, keys, preferred_element_type=jnp.float32) * att_scale
    )
    head_count, query_count, key_count = scores.shape
    shaped = jnp.exp(scores).reshape(
        head_count, query_count // group_rows, group_rows, key_count // TOK_TILE, TOK_TILE
    )
    shaped = shaped * tile_mask[None, :, None, :, None]
    return shaped.reshape(head_count, query_count, key_count)


def per_device(tokens, mod_shift, mod_scale, mod_gate, qkv_weight, out_weight, teacher, slot_tiles):
    tok_rows = tokens.shape[0]
    local_tiles = tok_rows // TOK_TILE
    head_count = out_weight.shape[0] // HD
    width_tiles = slot_tiles.shape[0] // (TT * TH)
    att_scale = 1.0 / math.sqrt(HD)
    normed = modulated_norm(tokens, mod_shift, mod_scale)
    projected = jnp.dot(normed, qkv_weight, preferred_element_type=jnp.float32).reshape(
        tok_rows, head_count, 3, HD
    )
    query_unit, query_factor = root_norm(projected[:, :, 0])
    key_unit, key_factor = root_norm(projected[:, :, 1])
    query_b = query_unit.astype(jnp.bfloat16)
    key_b = key_unit.astype(jnp.bfloat16)
    value_b = projected[:, :, 2].astype(jnp.bfloat16)
    all_keys, all_values = (
        lax.all_gather(key_b, "tile", axis=0, tiled=True),
        lax.all_gather(value_b, "tile", axis=0, tiled=True),
    )
    my_slots = lax.axis_index("tile") * local_tiles + jnp.arange(local_tiles, dtype=jnp.int32)
    my_tiles = tiles_of(slot_tiles, my_slots)
    tile_mask = near_tiles(my_tiles, slot_tiles, width_tiles)
    exp_scores = masked_exp(query_b, all_keys, tile_mask, TOK_TILE)
    totals = jnp.sum(exp_scores, -1)
    att_probs = exp_scores / totals[:, :, None]
    probs_b = att_probs.astype(jnp.bfloat16)
    attended = jnp.einsum(
        "hqk,khd->qhd", probs_b, all_values, preferred_element_type=jnp.float32
    ).astype(jnp.bfloat16)
    flat_att = attended.reshape(tok_rows, head_count * HD)
    partial_branch = jnp.dot(flat_att, out_weight, preferred_element_type=jnp.float32)
    whole_branch = lax.psum(partial_branch, "head")
    residual = LOSS_WEIGHT * (mod_gate * whole_branch - teacher.astype(jnp.float32))
    grad_branch = (mod_gate * residual).astype(jnp.bfloat16)
    contract_rows = (((0,), (0,)), ((), ()))
    out_term = lax.dot_general(
        flat_att, grad_branch, contract_rows, preferred_element_type=jnp.float32
    )
    grad_att = lax.dot_general(
        grad_branch, out_weight, (((1,), (1,)), ((), ())), preferred_element_type=jnp.float32
    )
    grad_att = grad_att.reshape(tok_rows, head_count, HD).astype(jnp.bfloat16)
    row_delta = jnp.sum(grad_att.astype(jnp.float32) * attended.astype(jnp.float32), -1)
    grad_probs = jnp.einsum(
        "qhd,khd->hqk", grad_att, all_values, preferred_element_type=jnp.float32
    )
    grad_scores = (att_probs * (grad_probs - row_delta.T[:, :, None])).astype(jnp.bfloat16)
    grad_query_unit = (
        jnp.einsum("hqk,khd->qhd", grad_scores, all_keys, preferred_element_type=jnp.float32)
        * att_scale
    )
    key_terms = (
        jnp.einsum("hqk,qhd->khd", grad_scores, query_b, preferred_element_type=jnp.float32)
        * att_scale
    )
    value_terms = jnp.einsum("hqk,qhd->khd", probs_b, grad_att, preferred_element_type=jnp.float32)
    grad_key_unit, grad_value = (
        lax.psum_scatter(key_terms, "tile", scatter_dimension=0, tiled=True),
        lax.psum_scatter(value_terms, "tile", scatter_dimension=0, tiled=True),
    )
    grad_query = root_norm_back(grad_query_unit, query_unit, query_factor)
    grad_key = root_norm_back(grad_key_unit, key_unit, key_factor)
    grad_qkv = (
        jnp.stack([grad_query, grad_key, grad_value], 2)
        .astype(jnp.bfloat16)
        .reshape(tok_rows, head_count * 3 * HD)
    )
    qkv_term = lax.dot_general(normed, grad_qkv, contract_rows, preferred_element_type=jnp.float32)
    qkv_grad, out_grad = (
        lax.psum_scatter(qkv_term, "tile", scatter_dimension=0, tiled=True),
        lax.psum_scatter(out_term, "tile", scatter_dimension=1, tiled=True),
    )
    return (qkv_grad, out_grad)


def solution(mesh):
    return jax.shard_map(
        per_device,
        mesh=mesh,
        in_specs=(
            P("tile", None),
            P(),
            P(),
            P(),
            P(None, "head"),
            P("head", None),
            P("tile", None),
            P(),
        ),
        out_specs=(P("tile", "head"), P("head", "tile")),
        check_vma=False,
    )
```

profile of v0, /device:TPU:1, one launch (start us, length us, event | category | flops | bytes accessed | tf_op | source)
XLA Modules:
  0.0 681.5 jit_solution(16059884396941234523)
XLA Ops:
  7.2 0.0 copy-start
  7.2 0.0 copy-start.8
  7.2 0.0 copy-start.11
  7.2 0.0 all-gather.4.cloned.1.call-start
  7.2 0.0 copy-start.2
  7.3 2.2 convert_reduce_fusion
  9.5 2.4 fusion.3
  11.9 0.0 copy-done.8
  11.9 0.0 copy-done
  11.9 0.0 copy-done.11
  11.9 0.0 copy-done.2
  12.0 0.0 copy-start.9
  12.0 1.7 fusion.47
  13.7 0.7 fusion.29
  14.4 0.0 all-gather.4.cloned.1.call-update
  14.4 0.0 all-gather.6.cloned.1.call-start
  14.4 0.7 slice.40
  15.1 0.0 all-gather.6.cloned.1.call-update
  15.1 0.0 all-reduce.2.cloned.1.call-start
  15.2 0.0 copy-done.9
  15.2 0.7 fusion.39
  18.7 0.1 mul.242
  18.8 57.1 %all-gather.4.cloned.1.call-done = bf16[6144,1,128]{0,2,1:T(8,128)(2,1)} async-done(((bf16[384,1,128]{0,2,1:T(8,128)(2,1)}), bf16[6144,1,128]{0,2,1:T(8,128)(2,1)}) %all-gather.4.cloned.1.call-update) | async-done | bytes 1572880 | tf_op jit(solution)/shard_map/all_gather | solution.py:81
  76.0 7.2 %fusion.49 = (f32[384]{0:T(512)S(1)}, f32[384,6144]{1,0:T(8,128)}) fusion(f32[6144]{0:T(1024)S(1)} %mul.243, bf16[6144,1,128]{0,2,1:T(8,128)(2,1)} %all-gather.4.cloned.1.call-done, f32[384,1,3,128]{0,3,2,1:T(8,128)S(1)} %bitcast.101, f32[384]{0:T(512)S(1)} %add_rsqrt_fusion.1), kind=kOutput, calls=%fused_computation.80 | convolution fusion | flops 611155584 | bytes 11234816 | tf_op jit(solution)/shard_map/qhd,khd->hqk/dot_general | solution.py:55
  83.2 52.0 %all-gather.6.cloned.1.call-done = bf16[6144,1,1,128]{0,3,2,1:T(8,128)(2,1)} async-done(((bf16[384,1,1,128]{0,3,2,1:T(8,128)(2,1)}), bf16[6144,1,1,128]{0,3,2,1:T(8,128)(2,1)}) %all-gather.6.cloned.1.call-update) | async-done | bytes 1572880 | tf_op jit(solution)/shard_map/all_gather | solution.py:82
  135.2 5.8 fusion.21
  141.0 0.0 copy-done.4
  141.0 0.0 copy-start.7
  141.0 2.9 fusion.35
  144.0 0.0 all-reduce.2.cloned.1.call-update
  144.0 0.0 reduce-scatter.5.cloned.1.call-start
  144.0 0.0 copy-done.7
  144.1 139.6 %all-reduce.2.cloned.1.call-done = f32[384,3072]{1,0:T(8,128)} async-done(((f32[384,3072]{1,0:T(8,128)}), f32[384,3072]{1,0:T(8,128)}) %all-reduce.2.cloned.1.call-update) | async-done | bytes 4718608 | tf_op jit(solution)/shard_map/psum | solution.py:96
  283.6 0.0 copy-start.5
  283.6 0.0 copy-start.10
  283.6 4.0 multiply_convert_fusion.1
  287.6 0.0 copy-done.5
  287.6 0.0 copy-start.3
  287.6 0.8 fusion.26
  288.5 0.6 copy-done.3
  289.0 0.0 copy-done.10
  289.0 4.6 multiply_convert_fusion
  293.7 0.0 copy-start.1
  293.7 2.2 copy-done.1
  295.9 2.6 fusion
  298.6 0.0 reduce-scatter.5.cloned.1.call-update
  298.6 0.0 reduce-scatter.7.cloned.1.call-start
  298.6 6.4 convolution_bitcast_fusion
  305.0 0.0 reduce-scatter.7.cloned.1.call-update
  305.0 0.2 reduce-scatter.11.cloned.1.call-start
  305.3 3.9 fusion.33
  309.2 0.0 reduce-scatter.11.cloned.1.call-update
  309.2 0.0 reduce-scatter.9.cloned.1.call-start
  309.2 81.2 %reduce-scatter.5.cloned.1.call-done = f32[384,1,128]{0,2,1:T(8,128)} async-done(((f32[6144,1,128]{0,2,1:T(8,128)}), f32[384,1,128]{0,2,1:T(8,128)}) %reduce-scatter.5.cloned.1.call-update) | async-done | bytes 196624 | tf_op jit(solution)/shard_map/reduce_scatter | solution.py:122
  390.4 0.0 copy-start.6
  390.4 4.4 multiply_reduce_fusion.1
  394.8 88.3 %reduce-scatter.7.cloned.1.call-done = f32[384,1,128]{0,2,1:T(8,128)} async-done(((f32[6144,1,128]{0,2,1:T(8,128)}), f32[384,1,128]{0,2,1:T(8,128)}) %reduce-scatter.7.cloned.1.call-update) | async-done | bytes 196624 | tf_op jit(solution)/shard_map/reduce_scatter | solution.py:123
  483.1 0.9 convert_bitcast_fusion
  484.1 0.0 copy-done.6
  484.1 0.1 fusion.31
  484.2 5.6 fusion.45
  489.8 0.0 reduce-scatter.9.cloned.1.call-update
  489.8 81.3 %reduce-scatter.11.cloned.1.call-done = f32[128,192]{0,1:T(8,128)} async-done(((f32[128,3072]{0,1:T(8,128)}), f32[128,192]{0,1:T(8,128)}) %reduce-scatter.11.cloned.1.call-update) | async-done | bytes 98320 | tf_op jit(solution)/shard_map/reduce_scatter | solution.py:135
  571.1 103.6 %reduce-scatter.9.cloned.1.call-done = f32[192,384]{1,0:T(8,128)} async-done(((f32[3072,384]{1,0:T(8,128)}), f32[192,384]{1,0:T(8,128)}) %reduce-scatter.9.cloned.1.call-update) | async-done | bytes 294928 | tf_op jit(solution)/shard_map/reduce_scatter | solution.py:134
  (12 shorter events, 0.2 us)
Async XLA Ops:
  7.2 4.8 copy-start
  7.2 4.7 copy-start.8
  7.2 4.7 copy-start.11
  7.2 68.8 %all-gather.4.cloned.1.call-start = ((), (), s32[]{:S(2)}) async-start(), calls=%async_computation.4 | async-start | bytes 1671168 | tf_op jit(solution)/shard_map/all_gather | solution.py:81
  7.2 4.7 copy-start.2
  12.0 3.2 copy-start.9
  14.4 120.8 %all-gather.6.cloned.1.call-start = ((), (), s32[]{:S(2)}) async-start(), calls=%async_computation.10 | async-start | bytes 1671168 | tf_op jit(solution)/shard_map/all_gather | solution.py:82
  15.1 268.5 %all-reduce.2.cloned.1.call-start = ((), (), s32[]{:S(2)}) async-start(), calls=%async_computation.5 | async-start | bytes 9437184 | tf_op jit(solution)/shard_map/psum | solution.py:96
  135.2 5.8 copy-start.4
  141.0 3.0 copy-start.7
  144.0 246.4 %reduce-scatter.5.cloned.1.call-start = ((), (), s32[]{:S(2)}) async-start(), calls=%async_computation.6 | async-start | bytes 3342336 | tf_op jit(solution)/shard_map/reduce_scatter | solution.py:122
  283.6 4.0 copy-start.5
  283.6 5.4 copy-start.10
  287.6 1.4 copy-start.3
  293.7 2.2 copy-start.1
  298.6 184.5 %reduce-scatter.7.cloned.1.call-start = ((), (), s32[]{:S(2)}) async-start(), calls=%async_computation.7 | async-start | bytes 3342336 | tf_op jit(solution)/shard_map/reduce_scatter | solution.py:123
  305.0 266.1 %reduce-scatter.11.cloned.1.call-start = ((), (), s32[]{:S(2)}) async-start(), calls=%async_computation.9 | async-start | bytes 1671168 | tf_op jit(solution)/shard_map/reduce_scatter | solution.py:135
  309.2 365.5 %reduce-scatter.9.cloned.1.call-start = ((), (), s32[]{:S(2)}) async-start(), calls=%async_computation.8 | async-start | bytes 5013504 | tf_op jit(solution)/shard_map/reduce_scatter | solution.py:134
  390.4 93.7 %copy-start.6 = (f32[384,1,128]{0,2,1:T(8,128)S(1)}, f32[384,1,128]{0,2,1:T(8,128)}, u32[]{:S(2)}) copy-start(f32[384,1,128]{0,2,1:T(8,128)} %reduce-scatter.5.cloned.1.call-done) | copy-start | bytes 589828
Sparse Core Ops, SparseCore 0:
  14.5 61.4 all-gather.3
  78.9 56.1 all-gather.5
  144.1 139.4 all-reduce.1
  298.7 91.6 reduce-scatter.4
  393.9 89.1 reduce-scatter.6
  487.1 83.9 reduce-scatter.10
  575.3 99.3 reduce-scatter.8
where the time goes:
time: 682 us
  waiting for transfers between devices  603 us (88%)
  matrix products  46 us (7%)
  between operations  17.2 us (3%)
  other arithmetic  11.1 us (2%)
    psum x1, waiting for transfers between devices, per_device(): whole_branch = lax.psum(partial_branch, 'head')  140 us
    reduce_scatter x1, waiting for transfers between devices, per_device(): lax.psum_scatter(qkv_term, 'tile', scatter_dimension=0, tiled=True)  104 us
    reduce_scatter x1, waiting for transfers between devices, per_device(): lax.psum_scatter(value_terms, 'tile', scatter_dimension=0, tiled=True)  88.3 us
    reduce_scatter x1, waiting for transfers between devices, per_device(): lax.psum_scatter(out_term, 'tile', scatter_dimension=1, tiled=True)  81.3 us
    reduce_scatter x1, waiting for transfers between devices, per_device(): lax.psum_scatter(key_terms, 'tile', scatter_dimension=0, tiled=True)  81.2 us
    all_gather x1, waiting for transfers between devices, per_device(): lax.all_gather(key_b, 'tile', axis=0, tiled=True)  57.1 us
    all_gather x1, waiting for transfers between devices, per_device(): lax.all_gather(value_b, 'tile', axis=0, tiled=True)  52 us
  transfers between devices with their start and end apart: 7, of which 7 were waited for; matrix products, arithmetic and copies ran while one was open for 4% of the time, Pallas kernels for 0%

commit v1 on v0

--- a/solution.py
+++ b/solution.py
@@ -93,7 +93,8 @@
     ).astype(jnp.bfloat16)
     flat_att = attended.reshape(tok_rows, head_count * HD)
     partial_branch = jnp.dot(flat_att, out_weight, preferred_element_type=jnp.float32)
-    whole_branch = lax.psum(partial_branch, "head")
+    parts = lax.all_gather(partial_branch, "head", axis=0, tiled=False)
+    whole_branch = parts.sum(axis=0)
     residual = LOSS_WEIGHT * (mod_gate * whole_branch - teacher.astype(jnp.float32))
     grad_branch = (mod_gate * residual).astype(jnp.bfloat16)
     contract_rows = (((0,), (0,)), ((), ()))

time: 682 us -> 937 us (1.37)
  waiting for transfers between devices: 603 us -> 833 us
  other arithmetic: 11.1 us -> 36.9 us
    all_gather x0 -> x1, waiting for transfers between devices: none -> 370 us  [per_device(): parts = lax.all_gather(partial_branch, 'head', axis=0, tiled=False)]
    psum x1 -> x0, waiting for transfers between devices: 140 us -> none  [per_device(): whole_branch = lax.psum(partial_branch, 'head')]
    reduce_sum x0 -> x1, other arithmetic: none -> 25.7 us  [per_device(): whole_branch = parts.sum(axis=0)]
  transfers between devices with their start and end apart: 7 -> 7, of which waited for: 7 -> 7; matrix products, arithmetic and copies ran while one was open for 4% -> 3% of each run, Pallas kernels for 0% -> 0%
where the time goes in v1:
time: 937 us
  waiting for transfers between devices  833 us (89%)
  matrix products  46.3 us (5%)
  other arithmetic  36.9 us (4%)
  between operations  17.2 us (2%)
    all_gather x1, waiting for transfers between devices, per_device(): parts = lax.all_gather(partial_branch, 'head', axis=0, tiled=False)  370 us
    reduce_scatter x1, waiting for transfers between devices, per_device(): lax.psum_scatter(qkv_term, 'tile', scatter_dimension=0, tiled=True)  104 us
    reduce_scatter x1, waiting for transfers between devices, per_device(): lax.psum_scatter(value_terms, 'tile', scatter_dimension=0, tiled=True)  88.4 us
    reduce_scatter x1, waiting for transfers between devices, per_device(): lax.psum_scatter(out_term, 'tile', scatter_dimension=1, tiled=True)  81.1 us
    reduce_scatter x1, waiting for transfers between devices, per_device(): lax.psum_scatter(key_terms, 'tile', scatter_dimension=0, tiled=True)  79.9 us
    all_gather x1, waiting for transfers between devices, per_device(): lax.all_gather(key_b, 'tile', axis=0, tiled=True)  57.1 us
    all_gather x1, waiting for transfers between devices, per_device(): lax.all_gather(value_b, 'tile', axis=0, tiled=True)  51.9 us
    reduce_sum x1, other arithmetic, per_device(): whole_branch = parts.sum(axis=0)  25.7 us
  transfers between devices with their start and end apart: 7, of which 7 were waited for; matrix products, arithmetic and copies ran while one was open for 3% of the time, Pallas kernels for 0%

profile of v1, /device:TPU:1, one launch (start us, length us, event | category | flops | bytes accessed | tf_op | source)
XLA Modules:
  0.0 937.0 jit_solution(5755387117305677894)
XLA Ops:
  7.2 0.0 copy-start
  7.2 0.0 copy-start.8
  7.2 0.0 copy-start.11
  7.2 0.0 all-gather.6.cloned.1.call-start
  7.2 0.0 copy-start.2
  7.3 2.2 convert_reduce_fusion
  9.5 2.4 fusion.3
  11.9 0.0 copy-done.8
  11.9 0.0 copy-done
  11.9 0.0 copy-done.11
  11.9 0.0 copy-done.2
  12.0 0.0 copy-start.9
  12.0 1.7 fusion.47
  13.7 0.7 fusion.29
  14.4 0.0 all-gather.6.cloned.1.call-update
  14.4 0.0 all-gather.8.cloned.1.call-start
  14.4 0.7 slice.40
  15.1 0.0 all-gather.8.cloned.1.call-update
  15.1 0.0 all-gather.10.cloned.1.call-start
  15.2 0.0 copy-done.9
  15.2 0.7 fusion.39
  18.8 0.1 mul.242
  18.8 57.1 %all-gather.6.cloned.1.call-done = bf16[6144,1,128]{0,2,1:T(8,128)(2,1)} async-done(((bf16[384,1,128]{0,2,1:T(8,128)(2,1)}), bf16[6144,1,128]{0,2,1:T(8,128)(2,1)}) %all-gather.6.cloned.1.call-update) | async-done | bytes 1572880 | tf_op jit(solution)/shard_map/all_gather | solution.py:81
  76.0 7.3 fusion.49
  83.3 51.9 %all-gather.8.cloned.1.call-done = bf16[6144,1,1,128]{0,3,2,1:T(8,128)(2,1)} async-done(((bf16[384,1,1,128]{0,3,2,1:T(8,128)(2,1)}), bf16[6144,1,1,128]{0,3,2,1:T(8,128)(2,1)}) %all-gather.8.cloned.1.call-update) | async-done | bytes 1572880 | tf_op jit(solution)/shard_map/all_gather | solution.py:82
  135.2 5.8 fusion.21
  141.0 0.0 copy-done.4
  141.0 0.0 copy-start.7
  141.0 3.0 fusion.35
  144.0 0.0 all-gather.10.cloned.1.call-update
  144.1 0.0 reduce-scatter.5.cloned.1.call-start
  144.1 0.0 copy-done.7
  144.1 369.8 %all-gather.10.cloned.1.call-done = f32[6144,3072]{1,0:T(8,128)} async-done(((f32[384,3072]{1,0:T(8,128)}), f32[6144,3072]{1,0:T(8,128)}) %all-gather.10.cloned.1.call-update) | async-done | bytes 75497488 | tf_op jit(solution)/shard_map/all_gather | solution.py:96
  514.0 25.7 %reduce_sum.96 = f32[384,3072]{1,0:T(8,128)} reduce(f32[16,384,3072]{2,1,0:T(8,128)} %bitcast.13, f32[]{:T(128)} %constant.101.clone.1), dimensions={0}, to_apply=%region_6.7 | reduce | flops 17694720 | bytes 80216064 | tf_op jit(solution)/shard_map/reduce_sum | solution.py:97
  539.7 0.0 copy-start.5
  539.7 0.0 copy-start.10
  539.7 4.0 multiply_convert_fusion.1
  543.7 0.0 copy-done.5
  543.7 0.0 copy-start.3
  543.7 0.8 fusion.26
  544.6 0.6 copy-done.3
  545.2 0.0 copy-done.10
  545.2 4.6 multiply_convert_fusion
  549.8 0.0 copy-start.1
  549.8 2.1 copy-done.1
  552.0 2.7 fusion
  554.7 0.0 reduce-scatter.5.cloned.1.call-update
  554.7 0.2 reduce-scatter.7.cloned.1.call-start
  555.0 6.4 convolution_bitcast_fusion
  561.4 0.0 reduce-scatter.7.cloned.1.call-update
  561.4 0.0 reduce-scatter.11.cloned.1.call-start
  561.4 3.9 fusion.33
  565.3 0.0 reduce-scatter.11.cloned.1.call-update
  565.3 0.0 reduce-scatter.9.cloned.1.call-start
  565.4 79.9 %reduce-scatter.5.cloned.1.call-done = f32[384,1,128]{0,2,1:T(8,128)} async-done(((f32[6144,1,128]{0,2,1:T(8,128)}), f32[384,1,128]{0,2,1:T(8,128)}) %reduce-scatter.5.cloned.1.call-update) | async-done | bytes 196624 | tf_op jit(solution)/shard_map/reduce_scatter | solution.py:123
  645.3 4.4 multiply_reduce_fusion.1
  649.7 88.4 %reduce-scatter.7.cloned.1.call-done = f32[384,1,128]{0,2,1:T(8,128)} async-done(((f32[6144,1,128]{0,2,1:T(8,128)}), f32[384,1,128]{0,2,1:T(8,128)}) %reduce-scatter.7.cloned.1.call-update) | async-done | bytes 196624 | tf_op jit(solution)/shard_map/reduce_scatter | solution.py:124
  738.1 0.9 convert_bitcast_fusion
  739.1 0.0 copy-done.6
  739.1 0.1 fusion.31
  739.2 5.6 fusion.45
  744.8 0.0 reduce-scatter.9.cloned.1.call-update
  744.8 81.1 %reduce-scatter.11.cloned.1.call-done = f32[128,192]{0,1:T(8,128)} async-done(((f32[128,3072]{0,1:T(8,128)}), f32[128,192]{0,1:T(8,128)}) %reduce-scatter.11.cloned.1.call-update) | async-done | bytes 98320 | tf_op jit(solution)/shard_map/reduce_scatter | solution.py:136
  825.9 104.2 %reduce-scatter.9.cloned.1.call-done = f32[192,384]{1,0:T(8,128)} async-done(((f32[3072,384]{1,0:T(8,128)}), f32[192,384]{1,0:T(8,128)}) %reduce-scatter.9.cloned.1.call-update) | async-done | bytes 294928 | tf_op jit(solution)/shard_map/reduce_scatter | solution.py:135
  (13 shorter events, 0.2 us)
Async XLA Ops:
  7.2 4.8 copy-start
  7.2 4.7 copy-start.8
  7.2 4.7 copy-start.11
  7.2 68.8 %all-gather.6.cloned.1.call-start = ((), (), s32[]{:S(2)}) async-start(), calls=%async_computation.4 | async-start | bytes 1671168 | tf_op jit(solution)/shard_map/all_gather | solution.py:81
  7.2 4.7 copy-start.2
  12.0 3.2 copy-start.9
  14.4 120.8 %all-gather.8.cloned.1.call-start = ((), (), s32[]{:S(2)}) async-start(), calls=%async_computation.9 | async-start | bytes 1671168 | tf_op jit(solution)/shard_map/all_gather | solution.py:82
  15.1 498.8 %all-gather.10.cloned.1.call-start = ((), (), s32[]{:S(2)}) async-start(), calls=%async_computation.10 | async-start | bytes 80216064 | tf_op jit(solution)/shard_map/all_gather | solution.py:96
  135.2 5.8 copy-start.4
  141.0 3.1 copy-start.7
  144.1 501.2 %reduce-scatter.5.cloned.1.call-start = ((), (), s32[]{:S(2)}) async-start(), calls=%async_computation.5 | async-start | bytes 3342336 | tf_op jit(solution)/shard_map/reduce_scatter | solution.py:123
  539.7 4.0 copy-start.5
  539.7 5.5 copy-start.10
  543.7 1.5 copy-start.3
  549.8 2.1 copy-start.1
  554.7 183.4 %reduce-scatter.7.cloned.1.call-start = ((), (), s32[]{:S(2)}) async-start(), calls=%async_computation.6 | async-start | bytes 3342336 | tf_op jit(solution)/shard_map/reduce_scatter | solution.py:124
  561.4 264.5 %reduce-scatter.11.cloned.1.call-start = ((), (), s32[]{:S(2)}) async-start(), calls=%async_computation.8 | async-start | bytes 1671168 | tf_op jit(solution)/shard_map/reduce_scatter | solution.py:136
  565.3 364.8 %reduce-scatter.9.cloned.1.call-start = ((), (), s32[]{:S(2)}) async-start(), calls=%async_computation.7 | async-start | bytes 5013504 | tf_op jit(solution)/shard_map/reduce_scatter | solution.py:135
  645.3 93.8 %copy-start.6 = (f32[384,1,128]{0,2,1:T(8,128)S(1)}, f32[384,1,128]{0,2,1:T(8,128)}, u32[]{:S(2)}) copy-start(f32[384,1,128]{0,2,1:T(8,128)} %reduce-scatter.5.cloned.1.call-done) | copy-start | bytes 589828
Sparse Core Ops, SparseCore 0:
  14.5 61.4 all-gather.5
  78.9 56.1 all-gather.7
  144.2 369.7 all-gather.9
  554.8 90.4 reduce-scatter.4
  648.8 89.3 reduce-scatter.6
  742.1 83.8 reduce-scatter.10
  830.1 99.9 reduce-scatter.8
